TPU v7x, 128 devices: a whole 4x4x4 slice. The times are simulated.
128 devices in a mesh: seq: 16 (over z, y), head: 8 (over x, core).
Axes of the slice: x: 4, y: 4, z: 4, core: 2. Of those that a mesh axis runs over, the one named last changes fastest.
Arguments:
- normed: bfloat16 [32, 8192], P(None, 'seq'), may hold values from -6 to 6
- qkv_weight: bfloat16 [8192, 10240], P('seq', 'head'), may hold values from -0.0625 to 0.0625
- out_weight: bfloat16 [8192, 8192], P('head', 'seq'), may hold values from -0.0625 to 0.0625
- kv_cache: bfloat16 [1024, 2, 128, 1024], P('seq', None, None, 'head'), may hold values from -160 to 160
- lengths: int32 [8], replicated, may hold values from 1 to 9344, as said below
- slot_request: int32 [1024], P('seq'), may hold values from 0 to 8, as said below
- slot_block: int32 [1024], P('seq'), may hold values from 0 to 72, as said below
- send_list: int32 [16, 16, 4], P('seq'), may hold values from 0 to 64, as said below
- recv_list: int32 [16, 16, 4], P('seq'), may hold values from 0 to 64, as said below
Outputs:
- projected: bfloat16 [32, 8192], P('head', 'seq')
- moved_cache: bfloat16 [1024, 2, 128, 1024], P('seq', None, None, 'head')
Inputs may be any that keep to these rules, and one draw needn't show every extreme that they name: `lengths`: every request has at least one block; a request with n blocks has each of the block numbers 0 to n - 1 in exactly one slot, and its length lies in ((n - 1) * 128, n * 128]. `slot_request`: 8 marks an empty slot. `slot_block`: 0 in empty slots. 64 marks an unused entry, and send_list[s, e, c] is unused exactly where recv_list[e, s, c] is; every owned slot is sent exactly once and no empty slot is sent; at most 4 blocks go from one device to another, and some device receives exactly 4 from every device; after the scale-in only half of the seq devices hold blocks. `recv_list`: 64 marks an unused entry; each slot of a device is filled at most once.
All inputs are finite; a program needn't handle non-finite values.
Results may differ from a plain program's by a relative error of at most 0.025.
Values may be sent and summed in bfloat16 or wider, within the bound.
A program may use at most 128 MiB of HBM per device.

v0:
```python
import jax
import jax.numpy as jnp
from jax import lax
from jax.sharding import PartitionSpec as P

HEADS = 64
KV_HEADS = 8
HEAD = 128
POS = 4
BLOCK = 128
rope_base = 500000.0
neg_large = -1e30


def rotate(values, positions):
    half_width = values.shape[-1] // 2
    frequencies = rope_base ** (
        -(jnp.arange(half_width, dtype=jnp.float32) * 2.0 / values.shape[-1])
    )
    angles = positions[..., None] * frequencies
    cosine_table = jnp.cos(angles)
    sine_table = jnp.sin(angles)
    lower_half = values[..., :half_width]
    upper_half = values[..., half_width:]
    return jnp.concatenate(
        [
            lower_half * cosine_table - upper_half * sine_table,
            upper_half * cosine_table + lower_half * sine_table,
        ],
        axis=-1,
    )


def body(
    normed,
    qkv_weight,
    out_weight,
    kv_cache,
    lengths,
    slot_request,
    slot_block,
    send_list,
    recv_list,
):
    group_size = HEADS // KV_HEADS
    scale_factor = HEAD ** (-0.5)
    requests = lengths.shape[0]
    slot_count = kv_cache.shape[0]
    full_rows = lax.all_gather(normed, "seq", axis=1, tiled=True)
    projected_qkv = jnp.dot(
        full_rows,
        lax.all_gather(qkv_weight, "seq", axis=0, tiled=True),
        preferred_element_type=jnp.float32,
    )
    projected_qkv = projected_qkv.reshape(requests, POS, -1, group_size + 2, HEAD)
    local_kv = projected_qkv.shape[2]
    positions = (lengths[:, None] + jnp.arange(POS, dtype=jnp.int32)[None, :]).astype(jnp.float32)
    queries = rotate(projected_qkv[:, :, :, :group_size], positions[:, :, None, None]).astype(
        jnp.bfloat16
    )
    keys_new = rotate(projected_qkv[:, :, :, group_size], positions[:, :, None]).astype(
        jnp.bfloat16
    )
    values_new = projected_qkv[:, :, :, group_size + 1].astype(jnp.bfloat16)
    flat_send = send_list.reshape(-1)
    outgoing = kv_cache[jnp.minimum(flat_send, slot_count - 1)]
    outgoing = outgoing.reshape((lax.axis_size("seq"), -1) + kv_cache.shape[1:])
    incoming = lax.all_to_all(outgoing, "seq", split_axis=0, concat_axis=0, tiled=True)
    incoming = incoming.reshape((-1,) + kv_cache.shape[1:])
    moved_cache = jnp.zeros_like(kv_cache).at[recv_list.reshape(-1)].set(incoming, mode="drop")
    slot_clip = jnp.minimum(slot_request, requests - 1)
    live_slot = slot_request < requests
    token_pos = slot_block[:, None] * BLOCK + jnp.arange(BLOCK, dtype=jnp.int32)[None, :]
    token_valid = (token_pos < lengths[slot_clip][:, None]) & live_slot[:, None]
    cache_view = kv_cache.reshape(slot_count, 2, BLOCK, local_kv, HEAD)
    gathered = queries[slot_clip]
    scores = (
        jnp.einsum(
            "sptgd,sbtd->stgpb", gathered, cache_view[:, 0], preferred_element_type=jnp.float32
        )
        * scale_factor
    )
    scores = jnp.where(token_valid[:, None, None, None, :], scores, neg_large)
    slot_max = jnp.max(scores, axis=-1)
    weights = jnp.where(
        token_valid[:, None, None, None, :], jnp.exp(scores - slot_max[..., None]), 0.0
    )
    slot_sum = jnp.sum(weights, axis=-1)
    slot_acc = jnp.einsum(
        "stgpb,sbtd->stgpd",
        weights.astype(jnp.bfloat16),
        cache_view[:, 1],
        preferred_element_type=jnp.float32,
    )
    flat_width = local_kv * group_size * POS
    slot_max_flat = slot_max.reshape(slot_count, flat_width)
    member = slot_request[:, None] == jnp.arange(requests, dtype=jnp.int32)[None, :]
    request_max = jnp.max(
        jnp.where(member[:, None, :], slot_max_flat[:, :, None], neg_large), axis=0
    ).T
    rescale = jnp.exp(slot_max_flat - request_max[slot_clip])
    member_float = member.astype(jnp.float32).T
    request_sum = jnp.dot(
        member_float,
        slot_sum.reshape(slot_count, flat_width) * rescale,
        precision=lax.Precision.HIGHEST,
    )
    scaled_acc = (slot_acc.reshape(slot_count, flat_width, HEAD) * rescale[:, :, None]).reshape(
        slot_count, flat_width * HEAD
    )
    request_acc = jnp.dot(member_float, scaled_acc, precision=lax.Precision.HIGHEST).reshape(
        requests, flat_width, HEAD
    )
    total_max = lax.pmax(request_max, "seq")
    adjust = jnp.exp(request_max - total_max)
    total_sum, total_acc = (
        lax.psum((request_sum * adjust).astype(jnp.bfloat16), "seq").astype(jnp.float32),
        lax.psum((request_acc * adjust[:, :, None]).astype(jnp.bfloat16), "seq").astype(
            jnp.float32
        ),
    )
    new_scores = (
        jnp.einsum("rptgd,rqtd->rtgpq", queries, keys_new, preferred_element_type=jnp.float32)
        * scale_factor
    )
    causal = jnp.arange(POS)[:, None] >= jnp.arange(POS)[None, :]
    new_scores = jnp.where(causal, new_scores, neg_large)
    cache_max = total_max.reshape(requests, local_kv, group_size, POS)
    top_max = jnp.maximum(cache_max, jnp.max(new_scores, axis=-1))
    carry_scale = jnp.exp(cache_max - top_max)
    new_weights = jnp.where(causal, jnp.exp(new_scores - top_max[..., None]), 0.0)
    denominator = total_sum.reshape(requests, local_kv, group_size, POS) * carry_scale + jnp.sum(
        new_weights, axis=-1
    )
    numerator = (
        total_acc.reshape(requests, local_kv, group_size, POS, HEAD) * carry_scale[..., None]
    )
    numerator = numerator + jnp.einsum(
        "rtgpq,rqtd->rtgpd",
        new_weights.astype(jnp.bfloat16),
        values_new,
        preferred_element_type=jnp.float32,
    )
    attended = (
        (numerator / denominator[..., None])
        .transpose(0, 3, 1, 2, 4)
        .reshape(requests * POS, -1)
        .astype(jnp.bfloat16)
    )
    projected = lax.psum_scatter(
        jnp.dot(attended, out_weight, preferred_element_type=jnp.float32).astype(jnp.bfloat16),
        "head",
        scatter_dimension=0,
        tiled=True,
    )
    return (projected, moved_cache)


def solution(mesh):
    placed = (
        P(None, "seq"),
        P("seq", "head"),
        P("head", "seq"),
        P("seq", None, None, "head"),
        P(),
        P("seq"),
        P("seq"),
        P("seq", None, None),
        P("seq", None, None),
    )
    return jax.shard_map(
        body,
        mesh=mesh,
        in_specs=placed,
        out_specs=(P("head", "seq"), P("seq", None, None, "head")),
        check_vma=False,
    )
```

profile of v0, /device:TPU:0, one launch (start us, length us, event | category | flops | bytes accessed | tf_op | source)
XLA Modules:
  0.0 363.6 jit_solution(1940336600849006869)
XLA Ops:
  8.8 5.3 %gather_fusion.2 = bf16[64,2,128,128]{3,2,1,0:T(8,128)(2,1)} fusion(bf16[64,2,128,128]{3,2,1,0:T(8,128)(2,1)} %param.12, s32[1024]{0:T(1024)S(1)} %pad_clamp_fusion), kind=kCustom, calls=%fused_computation.2 | custom fusion | bytes 8388864 | tf_op jit(solution)/shard_map/gather | solution.py:66
  14.1 8.2 %all-to-all-start = ((bf16[16,4,2,128,128]{4,3,2,1,0:T(8,128)(2,1)}), bf16[16,4,2,128,128]{4,3,2,1,0:T(8,128)(2,1)}, u32[]{:S(2)}, u32[]{:S(2)}) async-start(bf16[16,4,2,128,128]{4,3,2,1,0:T(8,128)(2,1)} %bitcast.134), calls=%async_computation | async-start | bytes 8388608 | tf_op jit(solution)/shard_map/all_to_all | solution.py:68
  22.4 5.2 %copy.111 = bf16[64,2,128,128]{3,2,0,1:T(8,128)(2,1)} copy(bf16[64,2,128,128]{3,2,1,0:T(8,128)(2,1)} %param.12) | data formatting | bytes 8388608 | tf_op args[3]
  30.3 4.8 %compare_select_fusion.3 = (s32[64]{0:T(128)S(1)}, s32[64]{0:T(128)S(1)}, s32[64]{0:T(128)S(1)}) fusion(s32[]{:T(128)} %bitcast.1, s32[]{:T(128)} %bitcast.2, s32[]{:T(128)} %bitcast.3, s32[]{:T(128)} %bitcast.4, s32[]{:T(128)} %bitcast.5, s32[]{:T(128)} %bitcast.6, s32[]{:T(128)} %bitcast.7, s32[]{:T(128)} %bitcast.8, s32[64]{0:T(128)S(1)} %copy-done.7, ...), kind=kLoop, calls=%fused_computation.87 | loop fusion | flops 1216 | bytes 1312 | tf_op jit(solution)/shard_map/gather | solution.py:74
  35.2 80.1 %all_gather.6 = bf16[32,8192]{1,0:T(8,128)(2,1)S(1)} all-gather(bf16[32,512]{1,0:T(8,128)(2,1)S(1)} %copy-done.6), channel_id=1, replica_groups=mesh['seq'=16,'head'=8] {'seq'}, dimensions={1}, use_global_device_ids=true | all-gather | bytes 557056 | tf_op jit(solution)/shard_map/all_gather | solution.py:49
  115.7 3.1 broadcast_in_dim.96
  118.8 11.8 %scatter_fusion = bf16[64,2,128,128]{3,2,1,0:T(8,128)(2,1)} fusion(bf16[64,2,128,128]{3,2,1,0:T(8,128)(2,1)} %broadcast_in_dim.96, s32[64]{0:T(128)S(1)} %fusion.49, bf16[64,2,128,128]{3,2,1,0:T(8,128)(2,1)} %bitcast.45), kind=kCustom, calls=%fused_computation.3 | custom fusion | bytes 12583168 | tf_op jit(solution)/shard_map/scatter | solution.py:70
  130.6 61.3 %all-gather.2.cloned.1.call-done = bf16[8192,1280]{1,0:T(8,128)(2,1)} async-done(((bf16[512,1280]{1,0:T(8,128)(2,1)}), bf16[8192,1280]{1,0:T(8,128)(2,1)}) %all-gather.2.cloned.1.call-update) | async-done | bytes 20971536 | tf_op jit(solution)/shard_map/all_gather | solution.py:52
  191.9 8.8 %fusion.56 = f32[32,1280]{1,0:T(8,128)S(1)} fusion(bf16[32,8192]{1,0:T(8,128)(2,1)S(1)} %all_gather.6, bf16[8192,1280]{1,0:T(8,128)(2,1)} %all-gather.2.cloned.1.call-done), kind=kOutput, calls=%fused_computation.106 | convolution fusion | flops 671088640 | bytes 21659648 | tf_op jit(solution)/shard_map/dot_general | solution.py:50
  201.6 2.9 fusion.54
  205.5 38.1 %pmax.7 = f32[8,32]{1,0:T(8,128)S(1)} all-reduce(f32[8,32]{1,0:T(8,128)S(1)} %bitcast.130), channel_id=1, replica_groups=mesh['seq'=16,'head'=8] {'seq'}, use_global_device_ids=true, to_apply=%region_2.3 | all-reduce | flops 256 | bytes 2048 | tf_op jit(solution)/shard_map/pmax | solution.py:114
  243.7 1.2 gather_fusion.1
  246.3 0.8 fusion.15
  247.0 2.3 fusion
  249.7 0.8 subtract_exponential_fusion
  250.9 1.8 fusion.7
  253.3 0.9 fusion.45
  254.2 0.8 copy.73
  255.2 0.8 fusion.11
  256.2 36.0 %psum.15 = bf16[8,8,4]{1,2,0:T(4,128)(2,1)S(1)} all-reduce(bf16[8,8,4]{1,2,0:T(4,128)(2,1)S(1)} %copy.79), channel_id=1, replica_groups=mesh['seq'=16,'head'=8] {'seq'}, use_global_device_ids=true, to_apply=%region_6.7 | all-reduce | flops 256 | bytes 1024 | tf_op jit(solution)/shard_map/psum | solution.py:117
  292.2 1.4 fusion.55
  293.8 36.9 %all-reduce.3.cloned.1.call-done = bf16[8,8,4,128]{3,1,2,0:T(8,128)(2,1)} async-done(((bf16[8,8,4,128]{3,1,2,0:T(8,128)(2,1)}), bf16[8,8,4,128]{3,1,2,0:T(8,128)(2,1)}) %all-reduce.3.cloned.1.call-update) | async-done | bytes 65552 | tf_op jit(solution)/shard_map/psum | solution.py:118
  330.7 1.1 fusion.8
  332.1 24.0 %all-reduce = bf16[32,512]{1,0:T(8,128)(2,1)S(1)} all-reduce(bf16[32,512]{1,0:T(8,128)(2,1)S(1)} %convolution_convert_fusion), channel_id=2, replica_groups=mesh['seq'=16,'head'=8] {'head'}, use_global_device_ids=true, to_apply=%region_8.9.clone | all-reduce | flops 16384 | bytes 65536
  (75 shorter events, 10.2 us)
Async XLA Ops:
  7.2 324.7 %copy-start = (bf16[1024,512]{1,0:T(8,128)(2,1)S(1)}, bf16[1024,512]{1,0:T(8,128)(2,1)}, u32[]{:S(2)}) copy-start(bf16[1024,512]{1,0:T(8,128)(2,1)} %param.11) | copy-start | bytes 3145732
  7.2 184.7 %all-gather.2.cloned.1.call-start = ((), (), s32[]{:S(2)}) async-start(), calls=%async_computation.1 | async-start | bytes 22282240 | tf_op jit(solution)/shard_map/all_gather | solution.py:52
  14.1 101.6 %all-to-all-start = ((bf16[16,4,2,128,128]{4,3,2,1,0:T(8,128)(2,1)}), bf16[16,4,2,128,128]{4,3,2,1,0:T(8,128)(2,1)}, u32[]{:S(2)}, u32[]{:S(2)}) async-start(bf16[16,4,2,128,128]{4,3,2,1,0:T(8,128)(2,1)} %bitcast.134), calls=%async_computation | async-start | bytes 8388608 | tf_op jit(solution)/shard_map/all_to_all | solution.py:68
  22.3 5.3 %copy-start.9 = (s32[1,16,4]{1,2,0:T(4,128)S(1)}, s32[1,16,4]{1,2,0:T(4,128)}, u32[]{:S(2)}) copy-start(s32[1,16,4]{1,2,0:T(4,128)} %param.17) | copy-start | bytes 772
  22.3 5.5 %copy-start.12 = (u32[128]{0:T(128)S(1)}, u32[128]{0:T(128)}, u32[]{:S(2)}) copy-start(u32[128]{0:T(128)} %constant.43) | copy-start | bytes 1540
  22.3 7.4 %copy-start.3 = (s32[8]{0:T(128)S(1)}, s32[8]{0:T(128)}, u32[]{:S(2)}) copy-start(s32[8]{0:T(128)} %param.13) | copy-start | bytes 100
  22.3 8.0 %copy-start.7 = (s32[64]{0:T(128)S(1)}, s32[64]{0:T(128)}, u32[]{:S(2)}) copy-start(s32[64]{0:T(128)} %param.14) | copy-start | bytes 772
  22.3 8.0 %copy-start.11 = (s32[64]{0:T(128)S(1)}, s32[64]{0:T(128)}, u32[]{:S(2)}) copy-start(s32[64]{0:T(128)} %param.15) | copy-start | bytes 772
  22.3 12.8 %copy-start.6 = (bf16[32,512]{1,0:T(8,128)(2,1)S(1)}, bf16[32,512]{1,0:T(8,128)(2,1)}, u32[]{:S(2)}) copy-start(bf16[32,512]{1,0:T(8,128)(2,1)} %param.9) | copy-start | bytes 98308
  22.4 308.4 %all-reduce.3.cloned.1.call-start = ((), (), s32[]{:S(2)}) async-start(), calls=%async_computation.2 | async-start | bytes 131072 | tf_op jit(solution)/shard_map/psum | solution.py:118
  29.1 101.5 %copy-start.8 = (f32[64]{0:T(128)}, f32[64]{0:T(128)S(1)}, u32[]{:S(2)}) copy-start(f32[64]{0:T(128)S(1)} %negate_power_fusion) | copy-start | bytes 772
  115.4 15.2 %copy-start.5 = (f32[8,4]{1,0:T(8,128)}, f32[8,4]{1,0:T(8,128)S(1)}, u32[]{:S(2)}) copy-start(f32[8,4]{1,0:T(8,128)S(1)} %add_convert_fusion.1) | copy-start | bytes 388
  200.8 0.8 copy-start.1
  200.9 0.8 copy-start.2
  244.9 2.1 copy-start.4
  249.7 43.9 %copy-start.10 = (pred[4,4]{1,0:T(4,128)(4,1)S(1)}, pred[4,4]{1,0:T(4,128)(4,1)}, u32[]{:S(2)}) copy-start(pred[4,4]{1,0:T(4,128)(4,1)} %iota_compare_fusion.3) | copy-start | bytes 52
Sparse Core Ops, SparseCore 0:
  10.1 181.6 all-gather.1
  253.4 77.2 all-reduce.2
where the time goes:
time: 365 us; the launch traced here: 364 us
  blocking collectives  178 us (49%)
  waiting for transfers between devices  98.9 us (27%)
  local copies, waits for them, and re-layouts  34.3 us (9%)
  matrix products  19.4 us (5%)
  between operations  15.1 us (4%)
  other arithmetic  9.38 us (3%)
  starting transfers between devices  8.26 us (2%)
    all_gather x1, blocking collectives, body(): full_rows = lax.all_gather(normed, 'seq', axis=1, tiled=True)  80.1 us
    all_gather x1, waiting for transfers between devices, body(): lax.all_gather(qkv_weight, 'seq', axis=0, tiled=True)  61.3 us
    pmax x1, blocking collectives, body(): total_max = lax.pmax(request_max, 'seq')  38.1 us
    psum x1, waiting for transfers between devices, body(): lax.psum((request_acc * adjust[:, :, None]).astype(jnp.bfloat16), 'seq')  36.9 us
    psum x1, blocking collectives, body(): lax.psum((request_sum * adjust).astype(jnp.bfloat16), 'seq')  36 us
    unnamed x1, blocking collectives  24 us
    scatter x1, local copies, waits for them, and re-layouts, body(): jnp.zeros_like(kv_cache).at[recv_list.reshape(-1)]  11.8 us
    dot_general x1, matrix products, body(): jnp.dot(full_rows, lax.all_gather(qkv_weight, 'seq', axis=0, tiled=True),...  8.79 us
  transfers between devices with their start and end apart: 3, of which 2 were waited for; matrix products, arithmetic and copies ran while one was open for 10% of the time, Pallas kernels for 0%

commit v1 on v0

--- a/solution.py
+++ b/solution.py
@@ -113,9 +113,12 @@
     )
     total_max = lax.pmax(request_max, "seq")
     adjust = jnp.exp(request_max - total_max)
+    watch_cube_by_axis = lambda target, axis_tag: jnp.sum(
+        jax.lax.all_gather(target, axis_tag), axis=0
+    )
     total_sum, total_acc = (
         lax.psum((request_sum * adjust).astype(jnp.bfloat16), "seq").astype(jnp.float32),
-        lax.psum((request_acc * adjust[:, :, None]).astype(jnp.bfloat16), "seq").astype(
+        watch_cube_by_axis((request_acc * adjust[:, :, None]).astype(jnp.bfloat16), "seq").astype(
             jnp.float32
         ),
     )

time: 365 us -> 341 us (0.934)
  waiting for transfers between devices: 98.9 us -> 76.6 us
    psum x1 -> x0, waiting for transfers between devices: 36.9 us -> none  [body(): lax.psum((request_acc * adjust[:, :, None]).astype(jnp.bfloat16), 'seq')]
    all_gather x1, waiting for transfers between devices: 61.3 us -> 75.9 us  [body(): lax.all_gather(qkv_weight, 'seq', axis=0, tiled=True)]
    unnamed x30 -> x40, local copies, waits for them, and re-layouts: 6.56 us -> 8.26 us
  transfers between devices with their start and end apart: 3 -> 3, of which waited for: 2 -> 1; matrix products, arithmetic and copies ran while one was open for 10% -> 17% of each run, Pallas kernels for 0% -> 0%
where the time goes in v1:
time: 341 us; the launch traced here: 340 us
  blocking collectives  180 us (53%)
  waiting for transfers between devices  76.6 us (22%)
  local copies, waits for them, and re-layouts  33.3 us (10%)
  matrix products  17.5 us (5%)
  between operations  15.1 us (4%)
  other arithmetic  9.55 us (3%)
  starting transfers between devices  8.26 us (2%)
    all_gather x1, blocking collectives, body(): full_rows = lax.all_gather(normed, 'seq', axis=1, tiled=True)  82.1 us
    all_gather x1, waiting for transfers between devices, body(): lax.all_gather(qkv_weight, 'seq', axis=0, tiled=True)  75.9 us
    pmax x1, blocking collectives, body(): total_max = lax.pmax(request_max, 'seq')  38.1 us
    psum x1, blocking collectives, body(): lax.psum((request_sum * adjust).astype(jnp.bfloat16), 'seq')  36 us
    unnamed x1, blocking collectives  23.6 us
    scatter x1, local copies, waits for them, and re-layouts, body(): jnp.zeros_like(kv_cache).at[recv_list.reshape(-1)]  11.7 us
    dot_general x1, matrix products, body(): jnp.dot(full_rows, lax.all_gather(qkv_weight, 'seq', axis=0, tiled=True),...  8.8 us
    unnamed x40, local copies, waits for them, and re-layouts  8.26 us
  transfers between devices with their start and end apart: 3, of which 1 were waited for; matrix products, arithmetic and copies ran while one was open for 17% of the time, Pallas kernels for 0%

profile of v1, /device:TPU:0, one launch (start us, length us, event | category | flops | bytes accessed | tf_op | source)
XLA Modules:
  0.0 340.2 jit_solution(8442556454350314085)
XLA Ops:
  7.2 0.7 all-gather.4.cloned.1.call-update
  7.9 0.7 broadcast_minimum_fusion
  8.8 5.2 %gather_fusion.2 = bf16[64,2,128,128]{3,2,1,0:T(8,128)(2,1)} fusion(bf16[64,2,128,128]{3,2,1,0:T(8,128)(2,1)} %param.12, s32[1024]{0:T(1024)S(1)} %pad_clamp_fusion), kind=kCustom, calls=%fused_computation.2 | custom fusion | bytes 8388864 | tf_op jit(solution)/shard_map/gather | solution.py:66
  14.0 8.2 %all-to-all-start = ((bf16[16,4,2,128,128]{4,3,2,1,0:T(8,128)(2,1)}), bf16[16,4,2,128,128]{4,3,2,1,0:T(8,128)(2,1)}, u32[]{:S(2)}, u32[]{:S(2)}) async-start(bf16[16,4,2,128,128]{4,3,2,1,0:T(8,128)(2,1)} %bitcast.135), calls=%async_computation | async-start | bytes 8388608 | tf_op jit(solution)/shard_map/all_to_all | solution.py:68
  22.3 5.3 %copy.113 = bf16[64,2,128,128]{3,2,0,1:T(8,128)(2,1)} copy(bf16[64,2,128,128]{3,2,1,0:T(8,128)(2,1)} %param.12) | data formatting | bytes 8388608 | tf_op args[3]
  28.3 4.9 %compare_select_fusion.3 = (s32[64]{0:T(128)S(1)}, s32[64]{0:T(128)S(1)}, s32[64]{0:T(128)S(1)}) fusion(s32[]{:T(128)} %bitcast.1, s32[]{:T(128)} %bitcast.2, s32[]{:T(128)} %bitcast.3, s32[]{:T(128)} %bitcast.4, s32[]{:T(128)} %bitcast.5, s32[]{:T(128)} %bitcast.6, s32[]{:T(128)} %bitcast.7, s32[]{:T(128)} %bitcast.8, s32[64]{0:T(128)S(1)} %copy-done.13, ...), kind=kLoop, calls=%fused_computation.89 | loop fusion | flops 1216 | bytes 1312 | tf_op jit(solution)/shard_map/gather | solution.py:74
  33.2 82.1 %all_gather.12 = bf16[32,8192]{1,0:T(8,128)(2,1)S(1)} all-gather(bf16[32,512]{1,0:T(8,128)(2,1)S(1)} %copy-done.12), channel_id=1, replica_groups=mesh['seq'=16,'head'=8] {'seq'}, dimensions={1}, use_global_device_ids=true | all-gather | bytes 557056 | tf_op jit(solution)/shard_map/all_gather | solution.py:49
  116.0 75.9 %all-gather.4.cloned.1.call-done = bf16[8192,1280]{1,0:T(8,128)(2,1)} async-done(((bf16[512,1280]{1,0:T(8,128)(2,1)}), bf16[8192,1280]{1,0:T(8,128)(2,1)}) %all-gather.4.cloned.1.call-update) | async-done | bytes 20971536 | tf_op jit(solution)/shard_map/all_gather | solution.py:52
  191.8 8.8 %fusion.56 = f32[32,1280]{1,0:T(8,128)S(1)} fusion(bf16[32,8192]{1,0:T(8,128)(2,1)S(1)} %all_gather.12, bf16[8192,1280]{1,0:T(8,128)(2,1)} %all-gather.4.cloned.1.call-done), kind=kOutput, calls=%fused_computation.108 | convolution fusion | flops 671088640 | bytes 21659648 | tf_op jit(solution)/shard_map/dot_general | solution.py:50
  201.6 2.9 fusion.54
  204.6 0.7 copy.65
  205.5 1.2 gather_fusion.1
  206.7 38.1 %pmax.7 = f32[8,32]{1,0:T(8,128)S(1)} all-reduce(f32[8,32]{1,0:T(8,128)S(1)} %bitcast.134), channel_id=1, replica_groups=mesh['seq'=16,'head'=8] {'seq'}, use_global_device_ids=true, to_apply=%region_2.3 | all-reduce | flops 256 | bytes 2048 | tf_op jit(solution)/shard_map/pmax | solution.py:114
  244.9 0.8 fusion.15
  245.7 2.3 fusion
  248.4 0.8 subtract_exponential_fusion
  249.5 2.3 fusion.7
  251.9 0.8 copy.79
  252.7 1.2 dynamic-slice
  254.7 3.1 broadcast_in_dim.96
  257.8 11.7 %scatter_fusion = bf16[64,2,128,128]{3,2,1,0:T(8,128)(2,1)} fusion(bf16[64,2,128,128]{3,2,1,0:T(8,128)(2,1)} %broadcast_in_dim.96, s32[64]{0:T(128)S(1)} %fusion.49, bf16[64,2,128,128]{3,2,1,0:T(8,128)(2,1)} %bitcast.46), kind=kCustom, calls=%fused_computation.3 | custom fusion | bytes 12583168 | tf_op jit(solution)/shard_map/scatter | solution.py:70
  271.0 36.0 %psum.7 = bf16[8,8,4]{1,2,0:T(4,128)(2,1)S(1)} all-reduce(bf16[8,8,4]{1,2,0:T(4,128)(2,1)S(1)} %copy.78), channel_id=1, replica_groups=mesh['seq'=16,'head'=8] {'seq'}, use_global_device_ids=true, to_apply=%region_6.7 | all-reduce | flops 256 | bytes 1024 | tf_op jit(solution)/shard_map/psum | solution.py:120
  307.1 1.4 bitcast_reduce_fusion
  309.1 23.6 %all-reduce = bf16[32,512]{1,0:T(8,128)(2,1)S(1)} all-reduce(bf16[32,512]{1,0:T(8,128)(2,1)S(1)} %convolution_convert_fusion), channel_id=3, replica_groups=mesh['seq'=16,'head'=8] {'head'}, use_global_device_ids=true, to_apply=%region_8.9.clone | all-reduce | flops 16384 | bytes 65536
  (86 shorter events, 6.6 us)
Async XLA Ops:
  7.2 301.7 %copy-start = (bf16[1024,512]{1,0:T(8,128)(2,1)S(1)}, bf16[1024,512]{1,0:T(8,128)(2,1)}, u32[]{:S(2)}) copy-start(bf16[1024,512]{1,0:T(8,128)(2,1)} %param.11) | copy-start | bytes 3145732
  7.2 184.7 %all-gather.4.cloned.1.call-start = ((), (), s32[]{:S(2)}) async-start(), calls=%async_computation.1 | async-start | bytes 22282240 | tf_op jit(solution)/shard_map/all_gather | solution.py:52
  14.0 240.6 %all-to-all-start = ((bf16[16,4,2,128,128]{4,3,2,1,0:T(8,128)(2,1)}), bf16[16,4,2,128,128]{4,3,2,1,0:T(8,128)(2,1)}, u32[]{:S(2)}, u32[]{:S(2)}) async-start(bf16[16,4,2,128,128]{4,3,2,1,0:T(8,128)(2,1)} %bitcast.135), calls=%async_computation | async-start | bytes 8388608 | tf_op jit(solution)/shard_map/all_to_all | solution.py:68
  22.2 5.4 %copy-start.5 = (s32[8]{0:T(128)S(1)}, s32[8]{0:T(128)}, u32[]{:S(2)}) copy-start(s32[8]{0:T(128)} %param.13) | copy-start | bytes 100
  22.2 6.1 %copy-start.13 = (s32[64]{0:T(128)S(1)}, s32[64]{0:T(128)}, u32[]{:S(2)}) copy-start(s32[64]{0:T(128)} %param.14) | copy-start | bytes 772
  22.3 6.1 %copy-start.17 = (s32[64]{0:T(128)S(1)}, s32[64]{0:T(128)}, u32[]{:S(2)}) copy-start(s32[64]{0:T(128)} %param.15) | copy-start | bytes 772
  22.3 10.9 %copy-start.12 = (bf16[32,512]{1,0:T(8,128)(2,1)S(1)}, bf16[32,512]{1,0:T(8,128)(2,1)}, u32[]{:S(2)}) copy-start(bf16[32,512]{1,0:T(8,128)(2,1)} %param.9) | copy-start | bytes 98308
  22.3 284.8 %all-gather.6.cloned.1.call-start = ((), (), s32[]{:S(2)}) async-start(), calls=%async_computation.2 | async-start | bytes 1114112 | tf_op jit(solution)/shard_map/all_gather | solution.py:117
  27.6 88.0 %copy-start.15 = (f32[64]{0:T(128)}, f32[64]{0:T(128)S(1)}, u32[]{:S(2)}) copy-start(f32[64]{0:T(128)S(1)} %negate_power_fusion) | copy-start | bytes 772
  115.4 0.6 copy-start.10
  200.8 0.8 copy-start.1
  200.8 0.8 copy-start.3
  244.8 0.9 copy-start.8
  244.8 0.8 copy-start.6
  257.7 11.7 %copy-start.9 = (f32[8,32]{1,0:T(8,128)S(1)}, f32[8,32]{1,0:T(8,128)}, u32[]{:S(2)}) copy-start(f32[8,32]{1,0:T(8,128)} %copy-done.8) | copy-start | bytes 3076
  257.7 12.1 %copy-start.7 = (f32[8,32]{1,0:T(8,128)S(1)}, f32[8,32]{1,0:T(8,128)}, u32[]{:S(2)}) copy-start(f32[8,32]{1,0:T(8,128)} %copy-done.6) | copy-start | bytes 3076
  257.7 12.1 %copy-start.14 = (s32[64]{0:T(128)S(1)}, s32[64]{0:T(128)}, u32[]{:S(2)}) copy-start(s32[64]{0:T(128)} %param.14) | copy-start | bytes 772
  257.7 12.5 %copy-start.11 = (f32[8,4]{1,0:T(8,128)S(1)}, f32[8,4]{1,0:T(8,128)}, u32[]{:S(2)}) copy-start(f32[8,4]{1,0:T(8,128)} %copy-done.10) | copy-start | bytes 388
  257.7 12.5 %copy-start.16 = (f32[64]{0:T(128)S(1)}, f32[64]{0:T(128)}, u32[]{:S(2)}) copy-start(f32[64]{0:T(128)} %copy-done.15) | copy-start | bytes 772
  257.8 12.7 %copy-start.2 = (bf16[8,4,1,8,64]{4,3,1,0,2:T(8,128)(2,1)S(1)}, bf16[8,4,1,8,64]{4,3,1,0,2:T(8,128)(2,1)}, u32[]{:S(2)}) copy-start(bf16[8,4,1,8,64]{4,3,1,0,2:T(8,128)(2,1)} %copy-done.1) | copy-start | bytes 98308
  257.8 12.7 %copy-start.4 = (bf16[8,4,1,8,64]{4,3,1,0,2:T(8,128)(2,1)S(1)}, bf16[8,4,1,8,64]{4,3,1,0,2:T(8,128)(2,1)}, u32[]{:S(2)}) copy-start(bf16[8,4,1,8,64]{4,3,1,0,2:T(8,128)(2,1)} %copy-done.3) | copy-start | bytes 98308
Sparse Core Ops, SparseCore 0:
  10.1 181.6 all-gather.3
  252.0 39.8 all-gather.5
